TPU v7x, 256 devices: a whole 4x4x8 slice. The times are simulated.
256 devices in a mesh: dp: 2 (over y_lo), seq: 128 (over x, y_hi, z, core).
Axes of the slice: x: 4, y: 4 (y_hi: 2, y_lo: 2; y = y_hi * 2 + y_lo), z: 8, core: 2. Of those that a mesh axis runs over, the one named last changes fastest.
Arguments:
- tokens: bfloat16 [2, 128, 512, 384], P('dp', 'seq'), may hold values from -6 to 6
- cotangent: bfloat16 [2, 128, 512, 384], P('dp', 'seq'), may hold values from -6 to 6
- wqkv_spatial: bfloat16 [384, 1152], replicated, may hold values from -12.5 to 12.5
- wo_spatial: bfloat16 [384, 384], replicated, may hold values from -0.3125 to 0.3125
- wqkv_temporal: bfloat16 [384, 1152], replicated, may hold values from -12.5 to 12.5
- wo_temporal: bfloat16 [384, 384], replicated, may hold values from -0.3125 to 0.3125
Outputs:
- token_grad: bfloat16 [2, 128, 512, 384], P('dp', 'seq')
- grad_wqkv_spatial: float32 [384, 1152], P(None, 'seq')
- grad_wo_spatial: float32 [384, 384], P(None, 'seq')
- grad_wqkv_temporal: float32 [384, 1152], P(None, 'seq')
- grad_wo_temporal: float32 [384, 384], P(None, 'seq')
All inputs are finite; a program needn't handle non-finite values.
Results may differ from a plain program's by a relative error of at most 0.015.
Values may be sent and summed in bfloat16 or wider, within the bound.
No kernel may reach another device: no remote copies, remote signals or barrier semaphores. Data moves between devices by JAX's collectives and lax.ppermute only.
A program may use at most 64 MiB of HBM per device.

v0:
```python
import jax
import jax.numpy as jnp
from jax import lax
from jax.sharding import PartitionSpec as P

HEADS = 6


def product(pattern, left, right):
    return jnp.einsum(pattern, left, right, preferred_element_type=jnp.float32)


def normalize(values):
    average = jnp.mean(values, -1, keepdims=True)
    centered = values - average
    spread = jnp.mean(centered * centered, -1, keepdims=True)
    inverse = lax.rsqrt(spread + 1e-06)
    return (centered * inverse, inverse)


def normalize_back(scaled, inverse, upstream):
    return inverse * (
        upstream
        - jnp.mean(upstream, -1, keepdims=True)
        - scaled * jnp.mean(upstream * scaled, -1, keepdims=True)
    )


def patterns(layout):
    key_layout = layout.replace("s", "t")
    batch_letters = "".join((letter for letter in layout if letter not in "she"))
    return (key_layout, batch_letters + "hst")


def attend_block(queries, key_rows, values, layout):
    key_layout, score_layout = patterns(layout)
    factor = queries.shape[-1] ** (-0.5)
    scores = product(layout + "," + key_layout + "->" + score_layout, queries, key_rows) * factor
    probs = jax.nn.softmax(scores, axis=-1).astype(jnp.bfloat16)
    output = product(score_layout + "," + key_layout + "->" + layout, probs, values).astype(
        jnp.bfloat16
    )
    return (output, probs)


def attend_grad(queries, key_rows, values, upstream, probs, layout):
    key_layout, score_layout = patterns(layout)
    factor = queries.shape[-1] ** (-0.5)
    prob_grad = product(layout + "," + key_layout + "->" + score_layout, upstream, values)
    weights = probs.astype(jnp.float32)
    score_grad = (
        weights * (prob_grad - jnp.sum(weights * prob_grad, -1, keepdims=True)) * factor
    ).astype(jnp.bfloat16)
    query_grad = product(score_layout + "," + key_layout + "->" + layout, score_grad, key_rows)
    key_grad = product(score_layout + "," + layout + "->" + key_layout, score_grad, queries)
    value_grad = product(score_layout + "," + layout + "->" + key_layout, probs, upstream)
    return (query_grad, key_grad, value_grad)


def split_heads(combined):
    shape = combined.shape
    parted = combined.reshape(shape[:-1] + (3, HEADS, shape[-1] // (3 * HEADS)))
    return (parted[..., 0, :, :], parted[..., 1, :, :], parted[..., 2, :, :])


def frame_rows(tensor):
    return tensor.reshape((-1,) + tensor.shape[2:])


def on_device(tokens, cotangent, wqkv_spatial, wo_spatial, wqkv_temporal, wo_temporal):
    clip_count, frame_local, patch_count, model_width = tokens.shape
    head_width = model_width // HEADS
    block_rows = min(512, patch_count)
    inputs = tokens.astype(jnp.float32)
    scaled_s, inverse_s = normalize(inputs)
    normed_s = scaled_s.astype(jnp.bfloat16)
    combined_s = jnp.dot(normed_s, wqkv_spatial, preferred_element_type=jnp.float32).astype(
        jnp.bfloat16
    )
    queries_s, keys_s, values_s = [frame_rows(member) for member in split_heads(combined_s)]
    output, probs = attend_block(queries_s, keys_s, values_s, "bshe")
    outputs_s = [output]
    probs_s = [probs]
    attended_s = jnp.concatenate(outputs_s, 1).reshape(tokens.shape)
    stream = (inputs + jnp.dot(attended_s, wo_spatial, preferred_element_type=jnp.float32)).astype(
        jnp.bfloat16
    )
    stream_t, upstream_out = (
        lax.all_to_all(stream, "seq", split_axis=2, concat_axis=1, tiled=True),
        lax.all_to_all(cotangent, "seq", split_axis=2, concat_axis=1, tiled=True),
    )
    scaled_t, inverse_t = normalize(stream_t.astype(jnp.float32))
    normed_t = scaled_t.astype(jnp.bfloat16)
    combined_t = jnp.dot(normed_t, wqkv_temporal, preferred_element_type=jnp.float32).astype(
        jnp.bfloat16
    )
    queries_t, keys_t, values_t = split_heads(combined_t)
    attended_t, probs_t = attend_block(queries_t, keys_t, values_t, "csphe")
    attended_t = attended_t.reshape(stream_t.shape)
    factor = (
        clip_count * frame_local * patch_count * lax.axis_size("dp") * lax.axis_size("seq")
    ) ** (-0.5)
    grad_wo_t = product("cfpd,cfpe->de", attended_t, upstream_out) * factor
    head_grad_t = (
        product("cfpe,de->cfpd", upstream_out, wo_temporal)
        .astype(jnp.bfloat16)
        .reshape(queries_t.shape)
    )
    query_grad, key_grad, value_grad = attend_grad(
        queries_t, keys_t, values_t, head_grad_t, probs_t, "csphe"
    )
    combined_grad_t = (
        jnp.concatenate([query_grad, key_grad, value_grad], 3)
        .astype(jnp.bfloat16)
        .reshape(combined_t.shape)
    )
    grad_wqkv_t = product("cfpd,cfpe->de", normed_t, combined_grad_t) * factor
    input_grad_t = product("cfpe,de->cfpd", combined_grad_t, wqkv_temporal)
    branch_t = normalize_back(scaled_t, inverse_t, input_grad_t).astype(jnp.bfloat16)
    branch_s = lax.all_to_all(branch_t, "seq", split_axis=1, concat_axis=2, tiled=True)
    stream_grad = (cotangent.astype(jnp.float32) + branch_s.astype(jnp.float32)).astype(
        jnp.bfloat16
    )
    grad_wo_s = product("cfpd,cfpe->de", attended_s, stream_grad) * factor
    head_grad_s = frame_rows(
        product("cfpe,de->cfpd", stream_grad, wo_spatial)
        .astype(jnp.bfloat16)
        .reshape(tokens.shape[:3] + (HEADS, head_width))
    )
    key_total = jnp.zeros(keys_s.shape, jnp.float32)
    value_total = jnp.zeros(values_s.shape, jnp.float32)
    query_parts = []
    for number, offset in enumerate(range(0, patch_count, block_rows)):
        query_grad, key_grad, value_grad = attend_grad(
            queries_s, keys_s, values_s, head_grad_s, probs_s[number], "bshe"
        )
        query_parts.append(query_grad)
        key_total = key_total + key_grad
        value_total = value_total + value_grad
    combined_grad_s = jnp.concatenate([jnp.concatenate(query_parts, 1), key_total, value_total], 2)
    combined_grad_s = combined_grad_s.astype(jnp.bfloat16).reshape(combined_s.shape)
    grad_wqkv_s = product("cfpd,cfpe->de", normed_s, combined_grad_s) * factor
    input_grad_s = product("cfpe,de->cfpd", combined_grad_s, wqkv_spatial)
    token_grad = (
        stream_grad.astype(jnp.float32) + normalize_back(scaled_s, inverse_s, input_grad_s)
    ).astype(jnp.bfloat16)
    gradients = (grad_wqkv_s, grad_wo_s, grad_wqkv_t, grad_wo_t)
    summed = (
        lax.psum(gradients[0].astype(jnp.bfloat16), "dp").astype(jnp.float32),
        lax.psum(gradients[1].astype(jnp.bfloat16), "dp").astype(jnp.float32),
        lax.psum(gradients[2].astype(jnp.bfloat16), "dp").astype(jnp.float32),
        lax.psum(gradients[3].astype(jnp.bfloat16), "dp").astype(jnp.float32),
    )
    shares = (
        lax.psum_scatter(summed[0], "seq", scatter_dimension=1, tiled=True),
        lax.psum_scatter(summed[1], "seq", scatter_dimension=1, tiled=True),
        lax.psum_scatter(summed[2], "seq", scatter_dimension=1, tiled=True),
        lax.psum_scatter(summed[3], "seq", scatter_dimension=1, tiled=True),
    )
    return (token_grad, shares[0], shares[1], shares[2], shares[3])


def solution(mesh):
    in_specs = (P("dp", "seq", None, None), P("dp", "seq", None, None), P(), P(), P(), P())
    out_specs = (
        P("dp", "seq", None, None),
        P(None, "seq"),
        P(None, "seq"),
        P(None, "seq"),
        P(None, "seq"),
    )
    return jax.shard_map(
        on_device, mesh=mesh, in_specs=in_specs, out_specs=out_specs, check_vma=False
    )
```

profile of v0, /device:TPU:8, one launch (start us, length us, event | category | flops | bytes accessed | tf_op | source)
XLA Modules:
  0.0 970.6 jit_solution(3480285741127583737)
XLA Ops:
  9.7 3.2 convolution_convert_fusion.1
  14.4 4.8 fusion.74
  19.3 3.7 divide_convert_fusion
  27.0 3.0 reduce.31
  31.1 15.4 %all-to-all-start = ((bf16[128,2,768]{2,1,0:T(2,128)(2,1)}), bf16[128,2,768]{2,1,0:T(2,128)(2,1)S(1)}, u32[]{:S(2)}, u32[]{:S(2)}) async-start(bf16[128,2,768]{2,1,0:T(2,128)(2,1)} %reshape.483), calls=%async_computation | async-start | bytes 786432 | tf_op jit(solution)/shard_map/all_to_all | solution.py:89
  47.0 3.0 reduce.32
  51.1 13.5 %all-to-all-done = bf16[128,2,768]{2,1,0:T(2,128)(2,1)S(1)} async-done(((bf16[128,2,768]{2,1,0:T(2,128)(2,1)}), bf16[128,2,768]{2,1,0:T(2,128)(2,1)S(1)}, u32[]{:S(2)}, u32[]{:S(2)}) %all-to-all-start) | async-done | bytes 393248 | tf_op jit(solution)/shard_map/all_to_all | solution.py:89
  65.3 6.2 all-to-all-start.1
  71.5 2.7 reshape.484
  75.7 8.4 multiply_reduce_fusion.2
  93.4 4.1 convert_reduce_fusion.1
  97.5 3.6 fusion.75
  106.1 2.7 fusion.57
  109.0 3.4 convolution_bitcast_fusion.4
  112.4 3.4 convolution_bitcast_fusion.3
  123.0 14.0 %all-to-all-start.2 = ((bf16[1,128,4,384]{3,2,0,1:T(4,128)(2,1)}), bf16[1,128,4,384]{3,2,0,1:T(4,128)(2,1)S(1)}, u32[]{:S(2)}, u32[]{:S(2)}) async-start(bf16[1,128,4,384]{3,2,0,1:T(4,128)(2,1)} %copy.103), calls=%async_computation.2 | async-start | bytes 786432 | tf_op jit(solution)/shard_map/all_to_all | solution.py:120
  141.5 13.6 %all-to-all-done.2 = bf16[1,128,4,384]{3,2,0,1:T(4,128)(2,1)S(1)} async-done(((bf16[1,128,4,384]{3,2,0,1:T(4,128)(2,1)}), bf16[1,128,4,384]{3,2,0,1:T(4,128)(2,1)S(1)}, u32[]{:S(2)}, u32[]{:S(2)}) %all-to-all-start.2) | async-done | bytes 393248 | tf_op jit(solution)/shard_map/all_to_all | solution.py:120
  159.0 3.7 fusion.56
  162.7 9.3 fusion.20
  172.0 9.2 fusion.21
  181.2 3.0 convolution_bitcast_fusion.1
  188.8 2.7 fusion.76
  194.5 64.9 %all-reduce.9.cloned.1.call-done = (bf16[384,1152]{0,1:T(8,128)(2,1)}, bf16[384,384]{0,1:T(8,128)(2,1)}, bf16[384,1152]{0,1:T(8,128)(2,1)}, bf16[384,384]{0,1:T(8,128)(2,1)}) async-done(((bf16[384,1152]{0,1:T(8,128)(2,1)}, bf16[384,384]{0,1:T(8,128)(2,1)}, bf16[384,1152]{0,1:T(8,128)(2,1)}, bf16[384,384]{0,1:T(8,128)(2,1)}), (bf16[384,1152]{0,1:T(8,128)(2,1)}, bf16[384,384]{0,1:T(8,128)(2,1)}, ...) | async-done | bytes 2359312 | tf_op jit(solution)/shard_map/psum | solution.py:149
  259.4 699.4 %all-reduce.10 = (f32[384,1152]{0,1:T(8,128)S(1)}, f32[384,384]{0,1:T(8,128)}, f32[384,1152]{0,1:T(8,128)}, f32[384,384]{0,1:T(8,128)}) all-reduce(bf16[384,1152]{0,1:T(8,128)(2,1)} %get-tuple-element.13, bf16[384,384]{0,1:T(8,128)(2,1)} %get-tuple-element.14, ...), channel_id=2, replica_groups=mesh['dp'=2,'seq'=128] {'seq'}, use_global_device_ids=true, to_apply=%region_15.0.clone | all-reduce | flops 1179648 | bytes 7077888
  (102 shorter events, 53.8 us)
Async XLA Ops:
  7.2 81.3 %copy-start = (bf16[384,1152]{1,0:T(8,128)(2,1)S(1)}, bf16[384,1152]{1,0:T(8,128)(2,1)}, u32[]{:S(2)}) copy-start(bf16[384,1152]{1,0:T(8,128)(2,1)} %param.10) | copy-start | bytes 2654212
  14.4 8.5 copy-start.5
  23.0 1.7 copy-start.1
  23.0 2.5 copy-start.2
  23.0 2.5 copy-start.14
  24.7 0.8 copy-start.3
  26.5 19.9 %copy-start.11 = (bf16[1,1,512,384]{3,2,1,0:T(8,128)(2,1)S(1)}, bf16[1,1,512,384]{3,2,1,0:T(8,128)(2,1)}, u32[]{:S(2)}) copy-start(bf16[1,1,512,384]{3,2,1,0:T(8,128)(2,1)} %param.7) | copy-start | bytes 1179652
  31.1 33.5 %all-to-all-start = ((bf16[128,2,768]{2,1,0:T(2,128)(2,1)}), bf16[128,2,768]{2,1,0:T(2,128)(2,1)S(1)}, u32[]{:S(2)}, u32[]{:S(2)}) async-start(bf16[128,2,768]{2,1,0:T(2,128)(2,1)} %reshape.483), calls=%async_computation | async-start | bytes 786432 | tf_op jit(solution)/shard_map/all_to_all | solution.py:89
  65.3 35.8 %all-to-all-start.1 = ((bf16[128,2,768]{2,1,0:T(2,128)(2,1)}), bf16[128,2,768]{2,1,0:T(2,128)(2,1)S(1)}, u32[]{:S(2)}, u32[]{:S(2)}) async-start(bf16[128,2,768]{2,1,0:T(2,128)(2,1)} %reshape.485), calls=%async_computation.1 | async-start | bytes 786432 | tf_op jit(solution)/shard_map/all_to_all | solution.py:90
  104.3 4.5 copy-start.8
  106.1 2.7 copy-start.7
  106.1 2.7 copy-start.20
  117.2 3.2 copy-start.18
  117.2 3.2 copy-start.19
  120.4 1.1 copy-start.12
  121.9 16.7 %copy-start.9 = (bf16[128,4,384]{0,2,1:T(8,128)(2,1)S(1)}, bf16[128,4,384]{0,2,1:T(8,128)(2,1)}, u32[]{:S(2)}) copy-start(bf16[128,4,384]{0,2,1:T(8,128)(2,1)} %copy-done.8) | copy-start | bytes 1179652
  123.0 16.8 %copy-start.17 = (bf16[128,4,384]{2,1,0:T(4,128)(2,1)S(1)}, bf16[128,4,384]{2,1,0:T(4,128)(2,1)}, u32[]{:S(2)}) copy-start(bf16[128,4,384]{2,1,0:T(4,128)(2,1)} %convert_element_type.248) | copy-start | bytes 1179652
  123.0 32.1 %all-to-all-start.2 = ((bf16[1,128,4,384]{3,2,0,1:T(4,128)(2,1)}), bf16[1,128,4,384]{3,2,0,1:T(4,128)(2,1)S(1)}, u32[]{:S(2)}, u32[]{:S(2)}) async-start(bf16[1,128,4,384]{3,2,0,1:T(4,128)(2,1)} %copy.103), calls=%async_computation.2 | async-start | bytes 786432 | tf_op jit(solution)/shard_map/all_to_all | solution.py:120
  137.0 122.5 %all-reduce.9.cloned.1.call-start = ((), (), s32[]{:S(2)}) async-start(), calls=%async_computation.3 | async-start | bytes 4718592 | tf_op jit(solution)/shard_map/psum | solution.py:149
  137.2 2.6 copy-start.13
  141.5 16.0 %copy-start.4 = (bf16[6,64,512]{2,1,0:T(8,128)(2,1)S(1)}, bf16[6,64,512]{2,1,0:T(8,128)(2,1)}, u32[]{:S(2)}) copy-start(bf16[6,64,512]{2,1,0:T(8,128)(2,1)} %copy-done.3) | copy-start | bytes 1179652
  156.0 3.0 copy-start.6
  181.2 3.0 copy-start.15
  181.2 3.0 copy-start.16
  (2 other events, 1.4 us)
Sparse Core Ops, SparseCore 0:
  186.4 73.0 all-reduce.8
where the time goes:
time: 979 us; the launch traced here: 971 us
  blocking collectives  699 us (71%)
  waiting for transfers between devices  92.1 us (9%)
  matrix products  64.3 us (7%)
  starting transfers between devices  35.7 us (4%)
  local copies, waits for them, and re-layouts  32 us (3%)
  other arithmetic  31 us (3%)
  between operations  16 us (2%)
    unnamed x1, blocking collectives  699 us
    psum x1, waiting for transfers between devices, on_device(): lax.psum(gradients[0].astype(jnp.bfloat16), 'dp').astype(jnp.float32)  64.9 us
    dot_general x18, matrix products, product(): return jnp.einsum(pattern, left, right, preferred_element_type=jnp.float32)  49.7 us
  transfers between devices with their start and end apart: 4, of which 3 were waited for; matrix products, arithmetic and copies ran while one was open for 5% of the time, Pallas kernels for 0%

commit v1 on v0

--- a/solution.py
+++ b/solution.py
@@ -146,7 +146,9 @@
     ).astype(jnp.bfloat16)
     gradients = (grad_wqkv_s, grad_wo_s, grad_wqkv_t, grad_wo_t)
     summed = (
-        lax.psum(gradients[0].astype(jnp.bfloat16), "dp").astype(jnp.float32),
+        jnp.sum(lax.all_gather(gradients[0].astype(jnp.bfloat16), "dp"), axis=0).astype(
+            jnp.float32
+        ),
         lax.psum(gradients[1].astype(jnp.bfloat16), "dp").astype(jnp.float32),
         lax.psum(gradients[2].astype(jnp.bfloat16), "dp").astype(jnp.float32),
         lax.psum(gradients[3].astype(jnp.bfloat16), "dp").astype(jnp.float32),

time: 979 us -> 1550 us (1.58)
  waiting for transfers between devices: 92.1 us -> 661 us
    unnamed x1 -> x4, waiting for transfers between devices: 0.02 us -> 572 us
    all_to_all x0 -> x1, blocking collectives: none -> 24.9 us  [on_device(): lax.all_to_all(branch_t, 'seq', split_axis=1, concat_axis=2, tiled=True)]
    unnamed x1, blocking collectives: 699 us -> 682 us
  transfers between devices with their start and end apart: 4 -> 5, of which waited for: 3 -> 5; matrix products, arithmetic and copies ran while one was open for 5% -> 3% of each run, Pallas kernels for 0% -> 0%
where the time goes in v1:
time: 1550 us
  blocking collectives  707 us (46%)
  waiting for transfers between devices  661 us (43%)
  matrix products  65.2 us (4%)
  other arithmetic  34.1 us (2%)
  starting transfers between devices  31.9 us (2%)
  local copies, waits for them, and re-layouts  30.7 us (2%)
  between operations  16 us (1%)
    unnamed x1, blocking collectives  682 us
    unnamed x4, waiting for transfers between devices  572 us
    psum x1, waiting for transfers between devices, on_device(): lax.psum(gradients[1].astype(jnp.bfloat16), 'dp').astype(jnp.float32)  54.6 us
    dot_general x18, matrix products, product(): return jnp.einsum(pattern, left, right, preferred_element_type=jnp.float32)  50.5 us
  transfers between devices with their start and end apart: 5, of which 5 were waited for; matrix products, arithmetic and copies ran while one was open for 3% of the time, Pallas kernels for 0%

profile of v1, /device:TPU:8, one launch (start us, length us, event | category | flops | bytes accessed | tf_op | source)
XLA Modules:
  0.0 1545.9 jit_solution(7995035240465291879)
XLA Ops:
  9.7 3.2 convolution_convert_fusion.1
  14.4 4.8 fusion.74
  19.3 3.7 divide_convert_fusion
  27.0 3.0 reduce.32
  31.1 25.7 %all-to-all-start = ((bf16[128,2,768]{2,1,0:T(2,128)(2,1)}), bf16[128,2,768]{2,1,0:T(2,128)(2,1)S(1)}, u32[]{:S(2)}, u32[]{:S(2)}) async-start(bf16[128,2,768]{2,1,0:T(2,128)(2,1)} %reshape.486), calls=%async_computation | async-start | bytes 786432 | tf_op jit(solution)/shard_map/all_to_all | solution.py:89
  57.3 3.0 reduce.33
  61.4 13.2 all-to-all-done
  74.6 6.2 all-to-all-start.1
  83.4 8.4 multiply_reduce_fusion.2
  91.8 7.1 all-to-all-done.1
  111.5 3.6 fusion.75
  119.3 3.4 convolution_bitcast_fusion.4
  122.7 3.4 convolution_bitcast_fusion.3
  129.3 24.9 %all_to_all.12 = bf16[1,128,4,384]{3,2,0,1:T(4,128)(2,1)S(1)} all-to-all(bf16[1,128,4,384]{3,2,0,1:T(4,128)(2,1)S(1)} %copy.110), channel_id=1, replica_groups=mesh['dp'=2,'seq'=128] {'seq'}, dimensions={1} | all-to-all | bytes 786432 | tf_op jit(solution)/shard_map/all_to_all | solution.py:120
  156.9 3.7 convolution_bitcast_fusion.1
  160.6 4.7 fusion.56
  165.3 9.5 fusion.20
  174.7 9.3 fusion.21
  188.3 4.1 convert_reduce_fusion.1
  201.0 14.5 all-gather.3.cloned.1.call-done
  220.3 2.7 fusion.76
  225.8 54.6 %all-reduce.12.cloned.1.call-done = (bf16[384,384]{0,1:T(8,128)(2,1)}, bf16[384,1152]{1,0:T(8,128)(2,1)}, bf16[384,384]{0,1:T(8,128)(2,1)}) async-done(((bf16[384,384]{0,1:T(8,128)(2,1)}, bf16[384,1152]{1,0:T(8,128)(2,1)}, bf16[384,384]{0,1:T(8,128)(2,1)}), (bf16[384,384]{0,1:T(8,128)(2,1)}, bf16[384,1152]{1,0:T(8,128)(2,1)}, bf16[384,384]{0,1:T(8,128)(2,1)})) %all-reduce.12.cloned.1.call-update) | async-done | bytes 1474576 | tf_op jit(solution)/shard_map/psum | solution.py:152
  280.5 681.8 %all-reduce.13 = (f32[384,384]{0,1:T(8,128)}, f32[384,1152]{1,0:T(8,128)S(1)}, f32[384,384]{0,1:T(8,128)}) all-reduce(bf16[384,384]{0,1:T(8,128)(2,1)} %get-tuple-element.32, bf16[384,1152]{1,0:T(8,128)(2,1)} %get-tuple-element.33, bf16[384,384]{0,1:T(8,128)(2,1)} %get-tuple-element.34), channel_id=4, replica_groups=mesh['dp'=2,'seq'=128] {'seq'}, use_global_device_ids=true, to_apply=%region_17.0.clone | all-reduce | flops 737280 | bytes 4423680
  965.8 571.7 %all-reduce.10.cloned.1.call-done = f32[384,1152]{0,1:T(8,128)} async-done(((f32[384,1152]{0,1:T(8,128)}), f32[384,1152]{0,1:T(8,128)}) %all-reduce.10.cloned.1.call-update) | async-done | bytes 1769488
  (116 shorter events, 59.8 us)
Async XLA Ops:
  7.2 99.1 %copy-start = (bf16[384,1152]{1,0:T(8,128)(2,1)S(1)}, bf16[384,1152]{1,0:T(8,128)(2,1)}, u32[]{:S(2)}) copy-start(bf16[384,1152]{1,0:T(8,128)(2,1)} %param.10) | copy-start | bytes 2654212
  14.4 8.5 copy-start.7
  23.0 1.7 copy-start.1
  23.0 2.5 copy-start.2
  23.0 2.5 copy-start.17
  26.5 30.2 %copy-start.12 = (bf16[1,1,512,384]{3,2,1,0:T(8,128)(2,1)S(1)}, bf16[1,1,512,384]{3,2,1,0:T(8,128)(2,1)}, u32[]{:S(2)}) copy-start(bf16[1,1,512,384]{3,2,1,0:T(8,128)(2,1)} %param.7) | copy-start | bytes 1179652
  31.1 43.5 %all-to-all-start = ((bf16[128,2,768]{2,1,0:T(2,128)(2,1)}), bf16[128,2,768]{2,1,0:T(2,128)(2,1)S(1)}, u32[]{:S(2)}, u32[]{:S(2)}) async-start(bf16[128,2,768]{2,1,0:T(2,128)(2,1)} %reshape.486), calls=%async_computation | async-start | bytes 786432 | tf_op jit(solution)/shard_map/all_to_all | solution.py:89
  74.6 24.3 %all-to-all-start.1 = ((bf16[128,2,768]{2,1,0:T(2,128)(2,1)}), bf16[128,2,768]{2,1,0:T(2,128)(2,1)S(1)}, u32[]{:S(2)}, u32[]{:S(2)}) async-start(bf16[128,2,768]{2,1,0:T(2,128)(2,1)} %reshape.488), calls=%async_computation.1 | async-start | bytes 786432 | tf_op jit(solution)/shard_map/all_to_all | solution.py:90
  80.8 134.7 %all-gather.3.cloned.1.call-start = ((), (), s32[]{:S(2)}) async-start(), calls=%async_computation.3 | async-start | bytes 2654208 | tf_op jit(solution)/shard_map/all_gather | solution.py:149
  101.5 1.9 copy-start.19
  101.5 2.6 copy-start.23
  106.2 5.2 copy-start.3
  115.0 2.7 copy-start.8
  115.0 2.7 copy-start.22
  122.7 3.4 copy-start.11
  126.1 1.4 copy-start.4
  126.1 1.4 copy-start.20
  126.1 1.4 copy-start.21
  188.3 92.2 %all-reduce.12.cloned.1.call-start = ((), (), s32[]{:S(2)}) async-start(), calls=%async_computation.5 | async-start | bytes 2949120 | tf_op jit(solution)/shard_map/psum | solution.py:152
  192.4 2.7 copy-start.10
  193.6 2.6 copy-start.16
  196.2 1.6 copy-start.6
  199.0 1338.5 %all-reduce.10.cloned.1.call-start = ((), (), s32[]{:S(2)}) async-start(), calls=%async_computation.4 | async-start | bytes 3538944
  219.0 1.3 copy-start.14
  (6 other events, 6.1 us)
Sparse Core Ops, SparseCore 0:
  188.4 27.0 all-gather.2
  218.2 62.1 all-reduce.11
  283.1 1254.3 all-reduce.9
